TPU v7x, 32 devices: a whole 2x2x4 slice. The times are simulated.
32 devices in a mesh: src: 4 (over y, core), help: 8 (over z, x).
Axes of the slice: x: 2, y: 2, z: 4, core: 2. Of those that a mesh axis runs over, the one named last changes fastest.
Arguments:
- tiles: int32 [2, 256], P(None, 'src'), may hold values from 0 to 31, as said below
- cell_slot: int32 [2, 32], replicated, may hold values from 0 to 31, as said below
- counts: int32 [32, 2], P(('src', 'help')), may hold values from 128 to 512, as said below
- src_points: bfloat16 [16384, 512], P(('src', 'help')), may hold values from -9 to 9
- tgt_points: bfloat16 [16384, 512], P(('src', 'help')), may hold values from -9 to 9
Outputs:
- source_potential: float32 [16384], P(('src', 'help'))
- target_potential: float32 [16384], P(('src', 'help'))
- transport: float32 [16384, 512], P(('src', 'help'))
Inputs may be any that keep to these rules, and one draw needn't show every extreme that they name: `tiles`: columns come in blocks of 64, block g for group g of 8 cells: a block's source cells have ids g * 8 to g * 8 + 7, its target cells lie in group g or in group g + 1 (group 4 - 1 is followed by group 0); no pair is listed twice, and every source cell and every target cell is named in some column. Each row is a permutation that keeps every cell in its group: cell c is stored at slot cell_slot[side, c], with cell_slot[side, c] // 8 equal to c // 8; slot k is rows k * 512 to k * 512 + 511 of the point arrays. `counts`: rows of a slot at and beyond its count are padding. Both ends of the range occur in each column.
All inputs are finite; a program needn't handle non-finite values.
Results may differ from a plain program's by a relative error of at most 0.004.
Values may be sent and summed in bfloat16 or wider, within the bound.
A program may use at most 192 MiB of HBM per device.

v0:
```python
import math
import jax
import jax.numpy as jnp
from jax import lax
from jax.sharding import PartitionSpec as P

ITERS = 2
EPSILON = 0.2
NEGATIVE = -1e30


def passed_along(array, axis, by):
    count = lax.axis_size(axis)
    return lax.ppermute(array, axis, [(i, (i + by) % count) for i in range(count)])


def combined_all(part, axis, combine):
    gathered = jax.tree.map(lambda a: lax.all_gather(a, axis), part)

    def take(source):
        return jax.tree.map(lambda a: lax.dynamic_index_in_dim(a, source, 0, False), gathered)

    return lax.fori_loop(
        1, lax.axis_size(axis), lambda source, state: combine(state, take(source)), take(0)
    )


def join_parts(first, second):
    highest = jnp.maximum(first[0], second[0])
    return (
        highest,
        first[1] * jnp.exp(first[0] - highest) + second[1] * jnp.exp(second[0] - highest),
    )


def lookup(cell_ids, slot_table):
    matches = cell_ids[:, None] == jnp.arange(slot_table.shape[0], dtype=jnp.int32)[None, :]
    return jnp.sum(jnp.where(matches, slot_table[None, :], 0), axis=1)


def half_norms(points, group_size, cell_rows):
    return 0.5 * jnp.sum(jnp.square(points.astype(jnp.float32)), axis=1).reshape(
        group_size, cell_rows
    )


def shards(tiles, cell_slot, counts, src_points, tgt_points):
    group_size = lax.axis_size("help")
    help_index = lax.axis_index("help")
    src_index = lax.axis_index("src")
    cell_rows = src_points.shape[0]
    width = src_points.shape[1]
    cost_scale = math.sqrt(width)
    source_all, source_counts = (src_points, counts)
    source_cells_held = 1
    own_points, own_counts = (
        lax.all_gather(tgt_points, "help", axis=0, tiled=True),
        lax.all_gather(counts, "help", axis=0, tiled=True),
    )
    next_points, next_counts = passed_along((own_points, own_counts), "src", -1)
    candidates = 2 * group_size
    positions = jnp.arange(cell_rows, dtype=jnp.int32)
    source_live = positions[None, :] < source_counts[:, 0:1]
    target_live = jnp.stack(
        [positions[None, :] < own_counts[:, 1:2], positions[None, :] < next_counts[:, 1:2]], axis=0
    )
    flat_live = target_live.reshape(candidates, cell_rows)
    source_half = half_norms(source_all, source_cells_held, cell_rows)
    target_half = jnp.stack(
        [
            half_norms(own_points, group_size, cell_rows),
            half_norms(next_points, group_size, cell_rows),
        ],
        axis=0,
    )
    flat_half = target_half.reshape(candidates, cell_rows)
    target_points = jnp.concatenate([own_points, next_points], axis=0)
    src_slot = lookup(tiles[0], cell_slot[0])
    tgt_slot = lookup(tiles[1], cell_slot[1])
    src_cells = src_slot % group_size
    tgt_cells = tgt_slot % group_size
    tgt_sides = jnp.where(tgt_slot // group_size == src_index, 0, 1)
    tgt_keys = tgt_sides * group_size + tgt_cells
    key_ids = jnp.arange(candidates, dtype=jnp.int32)
    is_mine = src_cells == help_index
    listed_keys = jnp.any(is_mine[:, None] & (tgt_keys[:, None] == key_ids[None, :]), axis=0)
    inner = lax.dot_general(
        src_points, target_points, (((1,), (1,)), ((), ())), preferred_element_type=jnp.float32
    )
    cost = (source_half[0][:, None] + flat_half.reshape(-1)[None, :] - inner) / cost_scale
    column_live = (flat_live & listed_keys[:, None]).reshape(-1)
    mask = source_live[0][:, None] & column_live[None, :]
    own_live = source_live[0]
    target_table = jnp.zeros((2, group_size, cell_rows), jnp.float32)
    source_table = jnp.zeros((source_cells_held, cell_rows), jnp.float32)
    source_own = jnp.zeros((cell_rows,), jnp.float32)
    target_own = jnp.zeros((cell_rows,), jnp.float32)
    for sweep in range(ITERS):
        row_flat_target = target_table.reshape(candidates, cell_rows)
        row_scores = jnp.where(
            mask, (row_flat_target.reshape(-1)[None, :] - cost) / EPSILON, NEGATIVE
        )
        part_max = jnp.max(row_scores, axis=1)
        part_sum = jnp.sum(jnp.exp(row_scores - part_max[:, None]), axis=1)
        row_source_own = jnp.where(own_live, -EPSILON * (part_max + jnp.log(part_sum)), 0.0)
        row_source_table = row_source_own[None, :]
        source_table = row_source_table
        source_own = row_source_own
        scores = jnp.where(mask, (source_table[0][:, None] - cost) / EPSILON, NEGATIVE)
        peaks = jnp.max(scores, axis=0)
        sums = jnp.sum(jnp.exp(scores - peaks[None, :]), axis=0)
        peaks = peaks.reshape(2, group_size, cell_rows)
        sums = sums.reshape(2, group_size, cell_rows)
        peaks, sums = combined_all((peaks, sums), "help", join_parts)
        carried_max, carried_sum = passed_along((peaks[1], sums[1]), "src", 1)
        joined = join_parts((peaks[0], sums[0]), (carried_max, carried_sum))
        target_group = jnp.where(target_live[0], -EPSILON * (joined[0] + jnp.log(joined[1])), 0.0)
        target_after = passed_along(target_group, "src", -1)
        col_target_table = jnp.stack([target_group, target_after], axis=0)
        col_target_own = target_group[help_index]
        target_table = col_target_table
        target_own = col_target_own
    flat_target = target_table.reshape(candidates, cell_rows)
    exponent = (source_table[0][:, None] + flat_target.reshape(-1)[None, :] - cost) / EPSILON
    weight = jnp.where(mask, jnp.exp(exponent), 0.0).astype(jnp.bfloat16)
    own_numerator = jnp.dot(weight, target_points, preferred_element_type=jnp.float32)
    own_denominator = jnp.sum(weight.astype(jnp.float32), axis=1)
    safe_total = jnp.where(own_live, own_denominator, 1.0)
    transport = jnp.where(own_live[:, None], own_numerator / safe_total[:, None], 0.0)
    return (source_own, target_own, transport)


def solution(mesh):
    in_specs = (
        P(None, "src"),
        P(),
        P(("src", "help"), None),
        P(("src", "help"), None),
        P(("src", "help"), None),
    )
    out_specs = (P(("src", "help")), P(("src", "help")), P(("src", "help"), None))
    return jax.shard_map(shards, mesh=mesh, in_specs=in_specs, out_specs=out_specs, check_vma=False)
```

profile of v0, /device:TPU:1, one launch (start us, length us, event | category | flops | bytes accessed | tf_op | source)
XLA Modules:
  0.0 362.8 jit_solution(11354192799630096327)
XLA Ops:
  7.9 75.9 %all-gather.3.cloned.1.call-done = bf16[4096,512]{1,0:T(8,128)(2,1)} async-done(((bf16[512,512]{1,0:T(8,128)(2,1)}), bf16[4096,512]{1,0:T(8,128)(2,1)}) %all-gather.3.cloned.1.call-update) | async-done | bytes 4194320 | tf_op jit(solution)/shard_map/all_gather | solution.py:57
  83.8 1.9 collective-permute-start.1
  85.7 14.5 %all-gather = s32[8,1,2]{2,1,0:T(1,128)S(1)} all-gather(s32[1,1,2]{2,1,0:T(1,128)} %bitcast.156), channel_id=1, replica_groups=mesh['src'=4,'help'=8] {'help'}, dimensions={0}, use_global_device_ids=true | all-gather | bytes 72 | tf_op jit(solution)/shard_map/all_gather | solution.py:58
  100.3 4.6 %collective-permute-start = (s32[8,2]{0,1:T(2,128)S(1)}, s32[8,2]{0,1:T(2,128)S(1)}, u32[]{:S(2)}, u32[]{:S(2)}) collective-permute-start(s32[8,2]{0,1:T(2,128)S(1)} %bitcast.162), channel_id=1, source_target_pairs={{0,24},{8,0},{16,8},{24,16},{1,25},{9,1},{17,9},{25,17},{2,26},{10... | collective-permute-start | bytes 200 | tf_op jit(solution)/shard_map/ppermute | solution.py:14
  107.3 1.2 multiply_reduce_fusion.2
  108.7 24.6 %collective-permute-done = s32[8,2]{0,1:T(2,128)S(1)} collective-permute-done((s32[8,2]{0,1:T(2,128)S(1)}, s32[8,2]{0,1:T(2,128)S(1)}, u32[]{:S(2)}, u32[]{:S(2)}) %collective-permute-start) | collective-permute-done | bytes 96 | tf_op jit(solution)/shard_map/ppermute | solution.py:14
  133.4 3.1 multiply_reduce_fusion.1
  136.5 4.4 %constant_dynamic-update-slice_fusion.1 = bf16[8192,512]{1,0:T(8,128)(2,1)} fusion(bf16[4096,512]{1,0:T(8,128)(2,1)} %all-gather.3.cloned.1.call-done), kind=kLoop, calls=%fused_computation.82 | loop fusion | bytes 8388608
  140.9 3.1 multiply_reduce_fusion
  144.0 4.4 %constant_dynamic-update-slice_fusion = bf16[8192,512]{1,0:T(8,128)(2,1)} fusion(bf16[8192,512]{1,0:T(8,128)(2,1)} %constant_dynamic-update-slice_fusion.1, bf16[4096,512]{1,0:T(8,128)(2,1)} %collective-permute-done.1), kind=kLoop, calls=%fused_computation.81 | loop fusion | bytes 8388608 | tf_op jit(solution)/shard_map/concatenate | solution.py:77
  148.4 10.4 %fusion.6 = (f32[512]{0:T(512)S(1)}, f32[512,8192]{0,1:T(8,128)S(1)}) fusion(pred[512]{0:T(512)(128)(4,1)S(1)} %iota_compare_fusion.6, pred[8192]{0:T(1024)(128)(4,1)S(1)} %and.81, bf16[8192,512]{1,0:T(8,128)(2,1)} %constant_dynamic-update-slice_fusion, bf16[512,512]{1,0:T(8,128)(2,1)S(1)} %copy-done.2, f32[8192]{0:T(1024)S(1)} %bitcast.153, ...), kind=kOutput, calls=%fused_computation.23 | convolution fusion | flops 4328521216 | bytes 25735680 | tf_op jit(solution)/shard_map/dot_general | solution.py:87
  158.9 7.0 %exponential_reduce_fusion.3 = f32[512]{0:T(512)S(1)} fusion(f32[512,8192]{0,1:T(8,128)S(1)} %get-tuple-element.304, f32[512]{0:T(512)S(1)} %get-tuple-element.303, pred[512]{0:T(512)(128)(4,1)S(1)} %iota_compare_fusion.6, pred[8192]{0:T(1024)(128)(4,1)S(1)} %and.81), kind=kLoop, calls=%fused_computation.22 | loop fusion | flops 25165312 | bytes 16790016 | tf_op jit(solution)/shard_map/reduce_sum | solution.py:104
  166.0 4.8 %fusion.7 = f32[8192]{0:T(1024)S(1)} fusion(f32[512,8192]{0,1:T(8,128)S(1)} %get-tuple-element.304, f32[512]{0:T(512)S(1)} %multiply_select_fusion.1, pred[512]{0:T(512)(128)(4,1)S(1)} %iota_compare_fusion.6, pred[8192]{0:T(1024)(128)(4,1)S(1)} %and.81), kind=kLoop, calls=%fused_computation.24 | loop fusion | flops 20963328 | bytes 16820736 | tf_op jit(solution)/shard_map/reduce_max | solution.py:110
  170.8 6.7 %exponential_reduce_fusion.2 = f32[8192]{0:T(1024)S(1)} fusion(f32[512,8192]{0,1:T(8,128)S(1)} %get-tuple-element.304, f32[8192]{0:T(1024)S(1)} %fusion.7, f32[512]{0:T(512)S(1)} %multiply_select_fusion.1, pred[512]{0:T(512)(128)(4,1)S(1)} %iota_compare_fusion.6, pred[8192]{0:T(1024)(128)(4,1)S(1)} %and.81), kind=kLoop, calls=%fused_computation.21 | loop fusion | flops 25157632 | bytes 16853504 | tf_op jit(solution)/shard_map/reduce_sum | solution.py:111
  177.5 24.8 %all_gather.21 = f32[8,2,8,512]{3,2,1,0:T(8,128)S(1)} all-gather(f32[1,2,8,512]{3,2,1,0:T(8,128)S(1)} %all_gather_reshape.13), channel_id=1, replica_groups=mesh['src'=4,'help'=8] {'help'}, dimensions={0}, use_global_device_ids=true | all-gather | bytes 294912 | tf_op jit(solution)/shard_map/all_gather | solution.py:18
  202.4 24.9 %all_gather.20 = f32[8,2,8,512]{3,2,1,0:T(8,128)S(1)} all-gather(f32[1,2,8,512]{3,2,1,0:T(8,128)S(1)} %all_gather_reshape.12), channel_id=1, replica_groups=mesh['src'=4,'help'=8] {'help'}, dimensions={0}, use_global_device_ids=true | all-gather | bytes 294912 | tf_op jit(solution)/shard_map/all_gather | solution.py:18
  227.7 11.7 %collective-permute-start.2 = (f32[8,512]{1,0:T(8,128)S(1)}, f32[8,512]{1,0:T(8,128)S(1)}, u32[]{:S(2)}, u32[]{:S(2)}) collective-permute-start(f32[8,512]{1,0:T(8,128)S(1)} %slice_bitcast_fusion.7), channel_id=1, source_target_pairs={{0,8},{8,16},{16,24},{24,0},{1,9},{9,17},{17,25},{25,1},{2,10},{10... | collective-permute-start | bytes 49160 | tf_op jit(solution)/shard_map/ppermute | solution.py:14
  239.5 0.8 collective-permute-done.2
  240.7 1.3 collective-permute-start.4
  242.0 2.3 collective-permute-done.4
  244.3 10.3 %fusion.8 = f32[512]{0:T(512)S(1)} fusion(f32[512,8192]{0,1:T(8,128)} %copy-done, f32[8192]{0:T(1024)S(1)} %bitcast.146, pred[512]{0:T(512)(128)(4,1)S(1)} %iota_compare_fusion.6, pred[8192]{0:T(1024)(128)(4,1)S(1)} %and.81), kind=kLoop, calls=%fused_computation.25 | loop fusion | flops 20971008 | bytes 16820736 | tf_op jit(solution)/shard_map/reduce_max | solution.py:103
  254.6 5.6 %exponential_reduce_fusion.1 = f32[512]{0:T(512)S(1)} fusion(f32[512,8192]{0,1:T(8,128)S(1)} %copy-done.1, f32[512]{0:T(512)S(1)} %fusion.8, f32[8192]{0:T(1024)S(1)} %bitcast.147, pred[512]{0:T(512)(128)(4,1)S(1)} %iota_compare_fusion.6, pred[8192]{0:T(1024)(128)(4,1)S(1)} %and.81), kind=kLoop, calls=%fused_computation.20 | loop fusion | flops 25165312 | bytes 16822784 | tf_op jit(solution)/shard_map/reduce_sum | solution.py:104
  260.2 4.8 %fusion.9 = f32[8192]{0:T(1024)S(1)} fusion(f32[512,8192]{0,1:T(8,128)S(1)} %copy-done.1, f32[512]{0:T(512)S(1)} %multiply_select_fusion, pred[512]{0:T(512)(128)(4,1)S(1)} %iota_compare_fusion.6, pred[8192]{0:T(1024)(128)(4,1)S(1)} %and.81), kind=kLoop, calls=%fused_computation.26 | loop fusion | flops 20963328 | bytes 16820736 | tf_op jit(solution)/shard_map/reduce_max | solution.py:110
  265.1 6.7 %exponential_reduce_fusion = f32[8192]{0:T(1024)S(1)} fusion(f32[512,8192]{0,1:T(8,128)S(1)} %copy-done.1, f32[8192]{0:T(1024)S(1)} %fusion.9, f32[512]{0:T(512)S(1)} %multiply_select_fusion, pred[512]{0:T(512)(128)(4,1)S(1)} %iota_compare_fusion.6, pred[8192]{0:T(1024)(128)(4,1)S(1)} %and.81), kind=kLoop, calls=%fused_computation.19 | loop fusion | flops 25157632 | bytes 16853504 | tf_op jit(solution)/shard_map/reduce_sum | solution.py:111
  271.8 25.1 %all_gather.23 = f32[8,2,8,512]{3,2,1,0:T(8,128)S(1)} all-gather(f32[1,2,8,512]{3,2,1,0:T(8,128)S(1)} %all_gather_reshape.15), channel_id=1, replica_groups=mesh['src'=4,'help'=8] {'help'}, dimensions={0}, use_global_device_ids=true | all-gather | bytes 294912 | tf_op jit(solution)/shard_map/all_gather | solution.py:18
  296.9 24.9 %all_gather.22 = f32[8,2,8,512]{3,2,1,0:T(8,128)S(1)} all-gather(f32[1,2,8,512]{3,2,1,0:T(8,128)S(1)} %all_gather_reshape.14), channel_id=1, replica_groups=mesh['src'=4,'help'=8] {'help'}, dimensions={0}, use_global_device_ids=true | all-gather | bytes 294912 | tf_op jit(solution)/shard_map/all_gather | solution.py:18
  322.2 11.8 %collective-permute-start.5 = (f32[8,512]{1,0:T(8,128)S(1)}, f32[8,512]{1,0:T(8,128)S(1)}, u32[]{:S(2)}, u32[]{:S(2)}) collective-permute-start(f32[8,512]{1,0:T(8,128)S(1)} %slice_bitcast_fusion.5), channel_id=1, source_target_pairs={{0,8},{8,16},{16,24},{24,0},{1,9},{9,17},{17,25},{25,1},{2,10},{10... | collective-permute-start | bytes 49160 | tf_op jit(solution)/shard_map/ppermute | solution.py:14
  334.1 0.8 collective-permute-done.5
  335.3 1.4 collective-permute-start.7
  337.3 1.6 collective-permute-done.7
  338.9 8.1 %convert_reduce_fusion = (f32[512]{0:T(512)S(1)}, bf16[512,8192]{0,1:T(8,128)(2,1)S(1)}) fusion(f32[512,8192]{0,1:T(8,128)} %copy-done, f32[8192]{0:T(1024)S(1)} %bitcast.148, f32[512]{0:T(512)S(1)} %multiply_select_fusion, pred[8192]{0:T(1024)(128)(4,1)S(1)} %and.81, pred[512]{0:T(512)(128)(4,1)S(1)} %iota_compare_fusion.6), kind=kLoop, calls=%fused_computation.18 | loop fusion | flops 33553920 | bytes 25211392 | tf_op jit(solution)/shard_map/reduce_sum | solution.py:127
  347.1 8.9 %fusion.10 = f32[512,512]{1,0:T(8,128)} fusion(bf16[512,8192]{0,1:T(8,128)(2,1)S(1)} %get-tuple-element.298, bf16[8192,512]{1,0:T(8,128)(2,1)} %constant_dynamic-update-slice_fusion, f32[512]{0:T(512)S(1)} %broadcast_select_fusion, pred[512]{0:T(512)(128)(4,1)S(1)} %iota_compare_fusion.6), kind=kOutput, calls=%fused_computation.30 | convolution fusion | flops 4295491584 | bytes 17828352 | tf_op jit(solution)/shard_map/dot_general | solution.py:126
  (79 shorter events, 6.4 us)
Async XLA Ops:
  7.2 141.3 %copy-start.2 = (bf16[512,512]{1,0:T(8,128)(2,1)S(1)}, bf16[512,512]{1,0:T(8,128)(2,1)}, u32[]{:S(2)}) copy-start(bf16[512,512]{1,0:T(8,128)(2,1)} %param.12) | copy-start | bytes 1572868
  7.2 76.6 %all-gather.3.cloned.1.call-start = ((), (), s32[]{:S(2)}) async-start(), calls=%async_computation | async-start | bytes 4718592 | tf_op jit(solution)/shard_map/all_gather | solution.py:57
  83.8 57.1 %collective-permute-start.1 = (bf16[4096,512]{1,0:T(8,128)(2,1)}, bf16[4096,512]{1,0:T(8,128)(2,1)}, u32[]{:S(2)}, u32[]{:S(2)}) collective-permute-start(bf16[4096,512]{1,0:T(8,128)(2,1)} %all-gather.3.cloned.1.call-done), channel_id=1, source_target_pairs={{0,24},{8,0},{16,8},{24,16},{1,25},{9,1},{17,9},{25,17},{2,26},{10... | collective-permute-start | bytes 12582920 | tf_op jit(solution)/shard_map/ppermute | solution.py:14
  100.3 33.0 %collective-permute-start = (s32[8,2]{0,1:T(2,128)S(1)}, s32[8,2]{0,1:T(2,128)S(1)}, u32[]{:S(2)}, u32[]{:S(2)}) collective-permute-start(s32[8,2]{0,1:T(2,128)S(1)} %bitcast.162), channel_id=1, source_target_pairs={{0,24},{8,0},{16,8},{24,16},{1,25},{9,1},{17,9},{25,17},{2,26},{10... | collective-permute-start | bytes 200 | tf_op jit(solution)/shard_map/ppermute | solution.py:14
  158.9 11.9 %copy-start = (f32[512,8192]{0,1:T(8,128)}, f32[512,8192]{0,1:T(8,128)S(1)}, u32[]{:S(2)}) copy-start(f32[512,8192]{0,1:T(8,128)S(1)} %get-tuple-element.304) | copy-start | bytes 50331652
  158.9 7.0 %copy-start.4 = (s32[1,2]{1,0:T(1,128)S(1)}, s32[1,2]{1,0:T(1,128)}, u32[]{:S(2)}) copy-start(s32[1,2]{1,0:T(1,128)} %param.11) | copy-start | bytes 28
  227.7 12.6 %collective-permute-start.2 = (f32[8,512]{1,0:T(8,128)S(1)}, f32[8,512]{1,0:T(8,128)S(1)}, u32[]{:S(2)}, u32[]{:S(2)}) collective-permute-start(f32[8,512]{1,0:T(8,128)S(1)} %slice_bitcast_fusion.7), channel_id=1, source_target_pairs={{0,8},{8,16},{16,24},{24,0},{1,9},{9,17},{17,25},{25,1},{2,10},{10... | collective-permute-start | bytes 49160 | tf_op jit(solution)/shard_map/ppermute | solution.py:14
  239.4 1.2 collective-permute-start.3
  240.7 3.6 collective-permute-start.4
  242.0 12.6 %copy-start.1 = (f32[512,8192]{0,1:T(8,128)S(1)}, f32[512,8192]{0,1:T(8,128)}, u32[]{:S(2)}) copy-start(f32[512,8192]{0,1:T(8,128)} %copy-done) | copy-start | bytes 50331652
  260.2 78.7 %copy-start.3 = (f32[512]{0:T(512)}, f32[512]{0:T(512)S(1)}, u32[]{:S(2)}) copy-start(f32[512]{0:T(512)S(1)} %multiply_select_fusion) | copy-start | bytes 6148
  322.2 12.7 %collective-permute-start.5 = (f32[8,512]{1,0:T(8,128)S(1)}, f32[8,512]{1,0:T(8,128)S(1)}, u32[]{:S(2)}, u32[]{:S(2)}) collective-permute-start(f32[8,512]{1,0:T(8,128)S(1)} %slice_bitcast_fusion.5), channel_id=1, source_target_pairs={{0,8},{8,16},{16,24},{24,0},{1,9},{9,17},{17,25},{25,1},{2,10},{10... | collective-permute-start | bytes 49160 | tf_op jit(solution)/shard_map/ppermute | solution.py:14
  334.1 1.2 collective-permute-start.6
  335.3 3.6 collective-permute-start.7
Sparse Core Ops, SparseCore 0:
  10.1 73.6 all-gather.2
where the time goes:
time: 363 us
  blocking collectives  114 us (31%)
  waiting for transfers between devices  107 us (29%)
  other arithmetic  63.1 us (17%)
  starting transfers between devices  32.9 us (9%)
  matrix products  19.3 us (5%)
  between operations  14.4 us (4%)
  local copies, waits for them, and re-layouts  11.2 us (3%)
    all_gather x4, blocking collectives, combined_all(): gathered = jax.tree.map(lambda a: lax.all_gather(a, axis), part)  99.8 us
    all_gather x1, waiting for transfers between devices, shards(): lax.all_gather(tgt_points, 'help', axis=0, tiled=True)  75.9 us
    ppermute x8, starting transfers between devices, passed_along(): lax.ppermute(array, axis, [(i, (i + by) % count) for i in range(count)])  32.8 us
    ppermute x8, waiting for transfers between devices, passed_along(): lax.ppermute(array, axis, [(i, (i + by) % count) for i in range(count)])  30.7 us
    all_gather x1, blocking collectives, shards(): lax.all_gather(counts, 'help', axis=0, tiled=True)  14.5 us
    reduce_sum x2, other arithmetic, shards(): sums = jnp.sum(jnp.exp(scores - peaks[None, :]), axis=0)  13.3 us
    reduce_sum x2, other arithmetic, shards(): part_sum = jnp.sum(jnp.exp(row_scores - part_max[:, None]), axis=1)  12.6 us
    dot_general x1, matrix products, shards(): lax.dot_general(src_points, target_points, (((1,), (1,)), ((), ())), pref...  10.4 us
  transfers between devices with their start and end apart: 9, of which 8 were waited for; matrix products, arithmetic and copies ran while one was open for 3% of the time, Pallas kernels for 0%

commit v1 on v0

--- a/solution.py
+++ b/solution.py
@@ -7,6 +7,23 @@
 ITERS = 2
 EPSILON = 0.2
 NEGATIVE = -1e30
+
+
+def joined_along(blocks, dim):
+    blocks = jnp.moveaxis(blocks, 0, dim)
+    dims = blocks.shape
+    return blocks.reshape(*dims[:dim], dims[dim] * dims[dim + 1], *dims[dim + 2 :])
+
+
+def ring_gather(x, axis, dim):
+    length = lax.axis_size(axis)
+    ahead = [(i, (i + 1) % length) for i in range(length)]
+    tiles = [x]
+    while len(tiles) < length:
+        tiles.append(lax.ppermute(tiles[-1], axis, ahead))
+    index = lax.axis_index(axis)
+    tiles = jnp.stack(tiles)[(index - jnp.arange(length)) % length]
+    return joined_along(tiles, dim)
 
 
 def passed_along(array, axis, by):
@@ -54,7 +71,7 @@
     source_all, source_counts = (src_points, counts)
     source_cells_held = 1
     own_points, own_counts = (
-        lax.all_gather(tgt_points, "help", axis=0, tiled=True),
+        ring_gather(tgt_points, "help", 0),
         lax.all_gather(counts, "help", axis=0, tiled=True),
     )
     next_points, next_counts = passed_along((own_points, own_counts), "src", -1)

time: 363 us -> 369 us (1.017)
  between operations: 14.4 us -> 1.04 us
  waiting for transfers between devices: 107 us -> 119 us
  starting transfers between devices: 32.9 us -> 41.4 us
    ppermute x0 -> x7, waiting for transfers between devices: none -> 84.7 us  [ring_gather(): tiles.append(lax.ppermute(tiles[-1], axis, ahead))]
    all_gather x1 -> x0, waiting for transfers between devices: 75.9 us -> none  [shards(): lax.all_gather(tgt_points, 'help', axis=0, tiled=True)]
    ppermute x8, starting transfers between devices: 32.8 us -> 39.3 us  [passed_along(): lax.ppermute(array, axis, [(i, (i + by) % count) for i in range(count)])]
    gather x0 -> x1, local copies, waits for them, and re-layouts: none -> 4.92 us  [ring_gather(): tiles = jnp.stack(tiles)[(index - jnp.arange(length)) % length]]
    concatenate x1 -> x0, local copies, waits for them, and re-layouts: 4.43 us -> none  [shards(): target_points = jnp.concatenate([own_points, next_points], axis=0)]
  transfers between devices with their start and end apart: 9 -> 15, of which waited for: 8 -> 14; matrix products, arithmetic and copies ran while one was open for 3% -> 3% of each run, Pallas kernels for 0% -> 0%
where the time goes in v1:
time: 369 us
  waiting for transfers between devices  119 us (32%)
  blocking collectives  111 us (30%)
  other arithmetic  61.3 us (17%)
  starting transfers between devices  41.4 us (11%)
  matrix products  20.8 us (6%)
  local copies, waits for them, and re-layouts  13.6 us (4%)
    all_gather x4, blocking collectives, combined_all(): gathered = jax.tree.map(lambda a: lax.all_gather(a, axis), part)  98.5 us
    ppermute x7, waiting for transfers between devices, ring_gather(): tiles.append(lax.ppermute(tiles[-1], axis, ahead))  84.7 us
    ppermute x8, starting transfers between devices, passed_along(): lax.ppermute(array, axis, [(i, (i + by) % count) for i in range(count)])  39.3 us
    ppermute x8, waiting for transfers between devices, passed_along(): lax.ppermute(array, axis, [(i, (i + by) % count) for i in range(count)])  34.2 us
    reduce_sum x2, other arithmetic, shards(): sums = jnp.sum(jnp.exp(scores - peaks[None, :]), axis=0)  13.3 us
    dot_general x1, matrix products, shards(): lax.dot_general(src_points, target_points, (((1,), (1,)), ((), ())), pref...  13.1 us
    all_gather x1, blocking collectives, shards(): lax.all_gather(counts, 'help', axis=0, tiled=True)  12.8 us
    reduce_sum x2, other arithmetic, shards(): part_sum = jnp.sum(jnp.exp(row_scores - part_max[:, None]), axis=1)  12.6 us
  transfers between devices with their start and end apart: 15, of which 14 were waited for; matrix products, arithmetic and copies ran while one was open for 3% of the time, Pallas kernels for 0%

profile of v1, /device:TPU:1, one launch (start us, length us, event | category | flops | bytes accessed | tf_op | source)
XLA Modules:
  0.0 368.6 jit_solution(17810984941617853211)
XLA Ops:
  2.8 14.9 %collective-permute-done.1 = bf16[512,512]{1,0:T(8,128)(2,1)S(1)} collective-permute-done((bf16[512,512]{1,0:T(8,128)(2,1)}, bf16[512,512]{1,0:T(8,128)(2,1)S(1)}, u32[]{:S(2)}, u32[]{:S(2)}) %collective-permute-start.1) | collective-permute-done | bytes 524320 | tf_op jit(solution)/shard_map/ppermute | solution.py:23
  17.6 14.9 %collective-permute-done.2 = bf16[512,512]{1,0:T(8,128)(2,1)S(1)} collective-permute-done((bf16[512,512]{1,0:T(8,128)(2,1)S(1)}, bf16[512,512]{1,0:T(8,128)(2,1)S(1)}, u32[]{:S(2)}, u32[]{:S(2)}) %collective-permute-start.2) | collective-permute-done | bytes 524320 | tf_op jit(solution)/shard_map/ppermute | solution.py:23
  32.6 14.1 %collective-permute-done.3 = bf16[512,512]{1,0:T(8,128)(2,1)S(1)} collective-permute-done((bf16[512,512]{1,0:T(8,128)(2,1)S(1)}, bf16[512,512]{1,0:T(8,128)(2,1)S(1)}, u32[]{:S(2)}, u32[]{:S(2)}) %collective-permute-start.3) | collective-permute-done | bytes 524320 | tf_op jit(solution)/shard_map/ppermute | solution.py:23
  46.6 13.2 %collective-permute-done.4 = bf16[512,512]{1,0:T(8,128)(2,1)S(1)} collective-permute-done((bf16[512,512]{1,0:T(8,128)(2,1)S(1)}, bf16[512,512]{1,0:T(8,128)(2,1)S(1)}, u32[]{:S(2)}, u32[]{:S(2)}) %collective-permute-start.4) | collective-permute-done | bytes 524320 | tf_op jit(solution)/shard_map/ppermute | solution.py:23
  61.7 10.5 %collective-permute-done.5 = bf16[512,512]{1,0:T(8,128)(2,1)S(1)} collective-permute-done((bf16[512,512]{1,0:T(8,128)(2,1)S(1)}, bf16[512,512]{1,0:T(8,128)(2,1)S(1)}, u32[]{:S(2)}, u32[]{:S(2)}) %collective-permute-start.5) | collective-permute-done | bytes 524320 | tf_op jit(solution)/shard_map/ppermute | solution.py:23
  74.8 9.0 %collective-permute-done.6 = bf16[512,512]{1,0:T(8,128)(2,1)S(1)} collective-permute-done((bf16[512,512]{1,0:T(8,128)(2,1)S(1)}, bf16[512,512]{1,0:T(8,128)(2,1)S(1)}, u32[]{:S(2)}, u32[]{:S(2)}) %collective-permute-start.6) | collective-permute-done | bytes 524320 | tf_op jit(solution)/shard_map/ppermute | solution.py:23
  86.2 8.2 %collective-permute-done.7 = bf16[512,512]{1,0:T(8,128)(2,1)S(1)} collective-permute-done((bf16[512,512]{1,0:T(8,128)(2,1)S(1)}, bf16[512,512]{1,0:T(8,128)(2,1)S(1)}, u32[]{:S(2)}, u32[]{:S(2)}) %collective-permute-start.7) | collective-permute-done | bytes 524320 | tf_op jit(solution)/shard_map/ppermute | solution.py:23
  95.3 4.9 %gather_fusion = bf16[8,512,512]{2,1,0:T(8,128)(2,1)} fusion(bf16[8,512,512]{2,1,0:T(8,128)(2,1)} %bitcast_dynamic-update-slice_fusion, s32[1024]{0:T(1024)S(1)} %pad_clamp_fusion), kind=kCustom, calls=%fused_computation | custom fusion | bytes 8388640 | tf_op jit(solution)/shard_map/gather | solution.py:25
  100.2 6.7 %collective-permute-start.8 = (bf16[4096,512]{1,0:T(8,128)(2,1)}, bf16[4096,512]{1,0:T(8,128)(2,1)}, u32[]{:S(2)}, u32[]{:S(2)}) collective-permute-start(bf16[4096,512]{1,0:T(8,128)(2,1)} %bitcast.165), channel_id=1, source_target_pairs={{0,24},{8,0},{16,8},{24,16},{1,25},{9,1},{17,9},{25,17},{2,26},{10... | collective-permute-start | bytes 12582920 | tf_op jit(solution)/shard_map/ppermute | solution.py:31
  106.9 12.8 %all-gather = s32[8,1,2]{2,1,0:T(1,128)S(1)} all-gather(s32[1,1,2]{2,1,0:T(1,128)S(1)} %bitcast.178), channel_id=1, replica_groups=mesh['src'=4,'help'=8] {'help'}, dimensions={0}, use_global_device_ids=true | all-gather | bytes 72 | tf_op jit(solution)/shard_map/all_gather | solution.py:75
  119.8 3.5 collective-permute-start
  124.0 29.6 %collective-permute-done = s32[8,2]{0,1:T(2,128)S(1)} collective-permute-done((s32[8,2]{0,1:T(2,128)S(1)}, s32[8,2]{0,1:T(2,128)S(1)}, u32[]{:S(2)}, u32[]{:S(2)}) %collective-permute-start) | collective-permute-done | bytes 96 | tf_op jit(solution)/shard_map/ppermute | solution.py:31
  153.7 3.1 multiply_reduce_fusion.1
  156.8 3.1 multiply_reduce_fusion
  160.0 13.1 %fusion.6 = (f32[512]{0:T(512)S(1)}, f32[512,8192]{0,1:T(8,128)S(1)}) fusion(pred[512]{0:T(512)(128)(4,1)S(1)} %iota_compare_fusion.6, pred[8192]{0:T(1024)(128)(4,1)S(1)} %and.99, bf16[512,512]{1,0:T(8,128)(2,1)S(1)} %copy-done.3, bf16[4096,512]{1,0:T(8,128)(2,1)} %collective-permute-done.8, bf16[4096,512]{1,0:T(8,128)(2,1)} %bitcast.166, ...), kind=kOutput, calls=%fused_computation.24 | convolution fusion | flops 4345298432 | bytes 25735680 | tf_op jit(solution)/shard_map/dot_general | solution.py:104
  173.1 7.0 %exponential_reduce_fusion.3 = f32[512]{0:T(512)S(1)} fusion(f32[512,8192]{0,1:T(8,128)S(1)} %get-tuple-element.304, f32[512]{0:T(512)S(1)} %get-tuple-element.303, pred[512]{0:T(512)(128)(4,1)S(1)} %iota_compare_fusion.6, pred[8192]{0:T(1024)(128)(4,1)S(1)} %and.99), kind=kLoop, calls=%fused_computation.23 | loop fusion | flops 25165312 | bytes 16790016 | tf_op jit(solution)/shard_map/reduce_sum | solution.py:121
  180.2 4.6 %fusion.7 = f32[8192]{0:T(1024)S(1)} fusion(f32[512,8192]{0,1:T(8,128)S(1)} %get-tuple-element.304, f32[512]{0:T(512)S(1)} %multiply_select_fusion.1, pred[512]{0:T(512)(128)(4,1)S(1)} %iota_compare_fusion.6, pred[8192]{0:T(1024)(128)(4,1)S(1)} %and.99), kind=kLoop, calls=%fused_computation.25 | loop fusion | flops 20963328 | bytes 16820736 | tf_op jit(solution)/shard_map/reduce_max | solution.py:127
  184.8 6.6 %exponential_reduce_fusion.2 = f32[8192]{0:T(1024)S(1)} fusion(f32[512,8192]{0,1:T(8,128)S(1)} %get-tuple-element.304, f32[8192]{0:T(1024)S(1)} %fusion.7, f32[512]{0:T(512)S(1)} %multiply_select_fusion.1, pred[512]{0:T(512)(128)(4,1)S(1)} %iota_compare_fusion.6, pred[8192]{0:T(1024)(128)(4,1)S(1)} %and.99), kind=kLoop, calls=%fused_computation.22 | loop fusion | flops 25157632 | bytes 16853504 | tf_op jit(solution)/shard_map/reduce_sum | solution.py:128
  191.5 24.8 %all_gather.17 = f32[8,2,8,512]{3,2,1,0:T(8,128)S(1)} all-gather(f32[1,2,8,512]{3,2,1,0:T(8,128)S(1)} %all_gather_reshape.13), channel_id=1, replica_groups=mesh['src'=4,'help'=8] {'help'}, dimensions={0}, use_global_device_ids=true | all-gather | bytes 294912 | tf_op jit(solution)/shard_map/all_gather | solution.py:35
  216.2 24.8 %all_gather.16 = f32[8,2,8,512]{3,2,1,0:T(8,128)S(1)} all-gather(f32[1,2,8,512]{3,2,1,0:T(8,128)S(1)} %all_gather_reshape.12), channel_id=1, replica_groups=mesh['src'=4,'help'=8] {'help'}, dimensions={0}, use_global_device_ids=true | all-gather | bytes 294912 | tf_op jit(solution)/shard_map/all_gather | solution.py:35
  241.5 11.9 %collective-permute-start.9 = (f32[8,512]{1,0:T(8,128)S(1)}, f32[8,512]{1,0:T(8,128)S(1)}, u32[]{:S(2)}, u32[]{:S(2)}) collective-permute-start(f32[8,512]{1,0:T(8,128)S(1)} %slice_bitcast_fusion.7), channel_id=1, source_target_pairs={{0,8},{8,16},{16,24},{24,0},{1,9},{9,17},{17,25},{25,1},{2,10},{10... | collective-permute-start | bytes 49160 | tf_op jit(solution)/shard_map/ppermute | solution.py:31
  254.6 2.4 collective-permute-start.11
  258.4 10.3 %fusion.8 = f32[512]{0:T(512)S(1)} fusion(f32[512,8192]{0,1:T(8,128)} %copy-done, f32[8192]{0:T(1024)S(1)} %bitcast.168, pred[512]{0:T(512)(128)(4,1)S(1)} %iota_compare_fusion.6, pred[8192]{0:T(1024)(128)(4,1)S(1)} %and.99), kind=kLoop, calls=%fused_computation.26 | loop fusion | flops 20971008 | bytes 16820736 | tf_op jit(solution)/shard_map/reduce_max | solution.py:120
  268.7 5.6 %exponential_reduce_fusion.1 = f32[512]{0:T(512)S(1)} fusion(f32[512,8192]{0,1:T(8,128)S(1)} %copy-done.1, f32[512]{0:T(512)S(1)} %fusion.8, f32[8192]{0:T(1024)S(1)} %bitcast.169, pred[512]{0:T(512)(128)(4,1)S(1)} %iota_compare_fusion.6, pred[8192]{0:T(1024)(128)(4,1)S(1)} %and.99), kind=kLoop, calls=%fused_computation.21 | loop fusion | flops 25165312 | bytes 16822784 | tf_op jit(solution)/shard_map/reduce_sum | solution.py:121
  274.4 4.8 %fusion.9 = f32[8192]{0:T(1024)S(1)} fusion(f32[512,8192]{0,1:T(8,128)S(1)} %copy-done.1, f32[512]{0:T(512)S(1)} %multiply_select_fusion, pred[512]{0:T(512)(128)(4,1)S(1)} %iota_compare_fusion.6, pred[8192]{0:T(1024)(128)(4,1)S(1)} %and.99), kind=kLoop, calls=%fused_computation.27 | loop fusion | flops 20963328 | bytes 16820736 | tf_op jit(solution)/shard_map/reduce_max | solution.py:127
  279.2 6.7 %exponential_reduce_fusion = f32[8192]{0:T(1024)S(1)} fusion(f32[512,8192]{0,1:T(8,128)S(1)} %copy-done.1, f32[8192]{0:T(1024)S(1)} %fusion.9, f32[512]{0:T(512)S(1)} %multiply_select_fusion, pred[512]{0:T(512)(128)(4,1)S(1)} %iota_compare_fusion.6, pred[8192]{0:T(1024)(128)(4,1)S(1)} %and.99), kind=kLoop, calls=%fused_computation.20 | loop fusion | flops 25157632 | bytes 16853504 | tf_op jit(solution)/shard_map/reduce_sum | solution.py:128
  285.9 24.4 %all_gather.19 = f32[8,2,8,512]{3,2,1,0:T(8,128)S(1)} all-gather(f32[1,2,8,512]{3,2,1,0:T(8,128)S(1)} %all_gather_reshape.15), channel_id=1, replica_groups=mesh['src'=4,'help'=8] {'help'}, dimensions={0}, use_global_device_ids=true | all-gather | bytes 294912 | tf_op jit(solution)/shard_map/all_gather | solution.py:35
  310.3 24.6 %all_gather.18 = f32[8,2,8,512]{3,2,1,0:T(8,128)S(1)} all-gather(f32[1,2,8,512]{3,2,1,0:T(8,128)S(1)} %all_gather_reshape.14), channel_id=1, replica_groups=mesh['src'=4,'help'=8] {'help'}, dimensions={0}, use_global_device_ids=true | all-gather | bytes 294912 | tf_op jit(solution)/shard_map/all_gather | solution.py:35
  335.3 12.6 %collective-permute-start.12 = (f32[8,512]{1,0:T(8,128)S(1)}, f32[8,512]{1,0:T(8,128)S(1)}, u32[]{:S(2)}, u32[]{:S(2)}) collective-permute-start(f32[8,512]{1,0:T(8,128)S(1)} %slice_bitcast_fusion.5), channel_id=1, source_target_pairs={{0,8},{8,16},{16,24},{24,0},{1,9},{9,17},{17,25},{25,1},{2,10},{10... | collective-permute-start | bytes 49160 | tf_op jit(solution)/shard_map/ppermute | solution.py:31
  349.1 2.1 collective-permute-start.14
  352.8 8.1 %convert_reduce_fusion = (f32[512]{0:T(512)S(1)}, bf16[512,8192]{0,1:T(8,128)(2,1)S(1)}) fusion(f32[512,8192]{0,1:T(8,128)} %copy-done, f32[8192]{0:T(1024)S(1)} %bitcast.170, f32[512]{0:T(512)S(1)} %multiply_select_fusion, pred[8192]{0:T(1024)(128)(4,1)S(1)} %and.99, pred[512]{0:T(512)(128)(4,1)S(1)} %iota_compare_fusion.6), kind=kLoop, calls=%fused_computation.19 | loop fusion | flops 33553920 | bytes 25211392 | tf_op jit(solution)/shard_map/reduce_sum | solution.py:144
  360.9 7.7 %fusion.12 = f32[512,512]{1,0:T(8,128)} fusion(bf16[512,8192]{0,1:T(8,128)(2,1)S(1)} %get-tuple-element.298, bf16[4096,512]{1,0:T(8,128)(2,1)} %collective-permute-done.8, bf16[4096,512]{1,0:T(8,128)(2,1)S(1)} %bitcast.167, f32[512]{0:T(512)S(1)} %broadcast_select_fusion, pred[512]{0:T(512)(128)(4,1)S(1)} %iota_compare_fusion.6), kind=kOutput, calls=%fused_computation.33 | convolution fusion | flops 4312268800 | bytes 17828352 | tf_op jit(solution)/shard_map/dot_general | solution.py:143
  (104 shorter events, 17.5 us)
Async XLA Ops:
  0.6 106.3 %copy-start.5 = (s32[1,2]{1,0:T(1,128)S(1)}, s32[1,2]{1,0:T(1,128)}, u32[]{:S(2)}) copy-start(s32[1,2]{1,0:T(1,128)} %param.11) | copy-start | bytes 28
  0.6 122.7 %copy-start.6 = (s32[2,64]{1,0:T(2,128)S(1)}, s32[2,64]{1,0:T(2,128)}, u32[]{:S(2)}) copy-start(s32[2,64]{1,0:T(2,128)} %param.9) | copy-start | bytes 1540
  0.7 122.7 %copy-start.7 = (s32[2,32]{1,0:T(2,128)S(1)}, s32[2,32]{1,0:T(2,128)}, u32[]{:S(2)}) copy-start(s32[2,32]{1,0:T(2,128)} %param.10) | copy-start | bytes 772
  0.7 122.9 %copy-start.3 = (bf16[512,512]{1,0:T(8,128)(2,1)S(1)}, bf16[512,512]{1,0:T(8,128)(2,1)}, u32[]{:S(2)}) copy-start(bf16[512,512]{1,0:T(8,128)(2,1)} %param.12) | copy-start | bytes 1572868
  0.7 17.0 %collective-permute-start.1 = (bf16[512,512]{1,0:T(8,128)(2,1)}, bf16[512,512]{1,0:T(8,128)(2,1)S(1)}, u32[]{:S(2)}, u32[]{:S(2)}) collective-permute-start(bf16[512,512]{1,0:T(8,128)(2,1)} %param.13), channel_id=1, source_target_pairs={{0,1},{1,2},{2,3},{3,4},{4,5},{5,6},{6,7},{7,0},{8,9},{9,10},{10,1... | collective-permute-start | bytes 1572872 | tf_op jit(solution)/shard_map/ppermute | solution.py:23
  17.6 14.9 %collective-permute-start.2 = (bf16[512,512]{1,0:T(8,128)(2,1)S(1)}, bf16[512,512]{1,0:T(8,128)(2,1)S(1)}, u32[]{:S(2)}, u32[]{:S(2)}) collective-permute-start(bf16[512,512]{1,0:T(8,128)(2,1)S(1)} %collective-permute-done.1), channel_id=1, source_target_pairs={{0,1},{1,2},{2,3},{3,4},{4,5},{5,6},{6,7},{7,0},{8,9},{9,10},{10,1... | collective-permute-start | bytes 1572872 | tf_op jit(solution)/shard_map/ppermute | solution.py:23
  32.6 14.1 %collective-permute-start.3 = (bf16[512,512]{1,0:T(8,128)(2,1)S(1)}, bf16[512,512]{1,0:T(8,128)(2,1)S(1)}, u32[]{:S(2)}, u32[]{:S(2)}) collective-permute-start(bf16[512,512]{1,0:T(8,128)(2,1)S(1)} %collective-permute-done.2), channel_id=1, source_target_pairs={{0,1},{1,2},{2,3},{3,4},{4,5},{5,6},{6,7},{7,0},{8,9},{9,10},{10,1... | collective-permute-start | bytes 1572872 | tf_op jit(solution)/shard_map/ppermute | solution.py:23
  46.6 13.2 %collective-permute-start.4 = (bf16[512,512]{1,0:T(8,128)(2,1)S(1)}, bf16[512,512]{1,0:T(8,128)(2,1)S(1)}, u32[]{:S(2)}, u32[]{:S(2)}) collective-permute-start(bf16[512,512]{1,0:T(8,128)(2,1)S(1)} %collective-permute-done.3), channel_id=1, source_target_pairs={{0,1},{1,2},{2,3},{3,4},{4,5},{5,6},{6,7},{7,0},{8,9},{9,10},{10,1... | collective-permute-start | bytes 1572872 | tf_op jit(solution)/shard_map/ppermute | solution.py:23
  59.9 12.4 %collective-permute-start.5 = (bf16[512,512]{1,0:T(8,128)(2,1)S(1)}, bf16[512,512]{1,0:T(8,128)(2,1)S(1)}, u32[]{:S(2)}, u32[]{:S(2)}) collective-permute-start(bf16[512,512]{1,0:T(8,128)(2,1)S(1)} %collective-permute-done.4), channel_id=1, source_target_pairs={{0,1},{1,2},{2,3},{3,4},{4,5},{5,6},{6,7},{7,0},{8,9},{9,10},{10,1... | collective-permute-start | bytes 1572872 | tf_op jit(solution)/shard_map/ppermute | solution.py:23
  72.2 11.5 %collective-permute-start.6 = (bf16[512,512]{1,0:T(8,128)(2,1)S(1)}, bf16[512,512]{1,0:T(8,128)(2,1)S(1)}, u32[]{:S(2)}, u32[]{:S(2)}) collective-permute-start(bf16[512,512]{1,0:T(8,128)(2,1)S(1)} %collective-permute-done.5), channel_id=1, source_target_pairs={{0,1},{1,2},{2,3},{3,4},{4,5},{5,6},{6,7},{7,0},{8,9},{9,10},{10,1... | collective-permute-start | bytes 1572872 | tf_op jit(solution)/shard_map/ppermute | solution.py:23
  83.7 10.7 %collective-permute-start.7 = (bf16[512,512]{1,0:T(8,128)(2,1)S(1)}, bf16[512,512]{1,0:T(8,128)(2,1)S(1)}, u32[]{:S(2)}, u32[]{:S(2)}) collective-permute-start(bf16[512,512]{1,0:T(8,128)(2,1)S(1)} %collective-permute-done.6), channel_id=1, source_target_pairs={{0,1},{1,2},{2,3},{3,4},{4,5},{5,6},{6,7},{7,0},{8,9},{9,10},{10,1... | collective-permute-start | bytes 1572872 | tf_op jit(solution)/shard_map/ppermute | solution.py:23
  100.2 56.6 %collective-permute-start.8 = (bf16[4096,512]{1,0:T(8,128)(2,1)}, bf16[4096,512]{1,0:T(8,128)(2,1)}, u32[]{:S(2)}, u32[]{:S(2)}) collective-permute-start(bf16[4096,512]{1,0:T(8,128)(2,1)} %bitcast.165), channel_id=1, source_target_pairs={{0,24},{8,0},{16,8},{24,16},{1,25},{9,1},{17,9},{25,17},{2,26},{10... | collective-permute-start | bytes 12582920 | tf_op jit(solution)/shard_map/ppermute | solution.py:31
  119.8 33.8 %collective-permute-start = (s32[8,2]{0,1:T(2,128)S(1)}, s32[8,2]{0,1:T(2,128)S(1)}, u32[]{:S(2)}, u32[]{:S(2)}) collective-permute-start(s32[8,2]{0,1:T(2,128)S(1)} %bitcast.184), channel_id=1, source_target_pairs={{0,24},{8,0},{16,8},{24,16},{1,25},{9,1},{17,9},{25,17},{2,26},{10... | collective-permute-start | bytes 200 | tf_op jit(solution)/shard_map/ppermute | solution.py:31
  173.1 11.7 %copy-start = (f32[512,8192]{0,1:T(8,128)}, f32[512,8192]{0,1:T(8,128)S(1)}, u32[]{:S(2)}) copy-start(f32[512,8192]{0,1:T(8,128)S(1)} %get-tuple-element.304) | copy-start | bytes 50331652
  241.5 12.7 %collective-permute-start.9 = (f32[8,512]{1,0:T(8,128)S(1)}, f32[8,512]{1,0:T(8,128)S(1)}, u32[]{:S(2)}, u32[]{:S(2)}) collective-permute-start(f32[8,512]{1,0:T(8,128)S(1)} %slice_bitcast_fusion.7), channel_id=1, source_target_pairs={{0,8},{8,16},{16,24},{24,0},{1,9},{9,17},{17,25},{25,1},{2,10},{10... | collective-permute-start | bytes 49160 | tf_op jit(solution)/shard_map/ppermute | solution.py:31
  253.3 1.2 collective-permute-start.10
  254.6 3.8 %collective-permute-start.11 = (f32[8,512]{1,0:T(8,128)S(1)}, f32[8,512]{1,0:T(8,128)S(1)}, u32[]{:S(2)}, u32[]{:S(2)}) collective-permute-start(f32[8,512]{1,0:T(8,128)S(1)} %fusion.26), channel_id=1, source_target_pairs={{0,24},{8,0},{16,8},{24,16},{1,25},{9,1},{17,9},{25,17},{2,26},{10... | collective-permute-start | bytes 49160 | tf_op jit(solution)/shard_map/ppermute | solution.py:31
  257.0 11.7 %copy-start.1 = (f32[512,8192]{0,1:T(8,128)S(1)}, f32[512,8192]{0,1:T(8,128)}, u32[]{:S(2)}) copy-start(f32[512,8192]{0,1:T(8,128)} %copy-done) | copy-start | bytes 50331652
  274.3 78.4 %copy-start.4 = (f32[512]{0:T(512)}, f32[512]{0:T(512)S(1)}, u32[]{:S(2)}) copy-start(f32[512]{0:T(512)S(1)} %multiply_select_fusion) | copy-start | bytes 6148
  335.3 13.5 %collective-permute-start.12 = (f32[8,512]{1,0:T(8,128)S(1)}, f32[8,512]{1,0:T(8,128)S(1)}, u32[]{:S(2)}, u32[]{:S(2)}) collective-permute-start(f32[8,512]{1,0:T(8,128)S(1)} %slice_bitcast_fusion.5), channel_id=1, source_target_pairs={{0,8},{8,16},{16,24},{24,0},{1,9},{9,17},{17,25},{25,1},{2,10},{10... | collective-permute-start | bytes 49160 | tf_op jit(solution)/shard_map/ppermute | solution.py:31
  347.9 1.2 collective-permute-start.13
  348.0 13.0 %copy-start.2 = (bf16[8,512,512]{2,1,0:T(8,128)(2,1)S(1)}, bf16[8,512,512]{2,1,0:T(8,128)(2,1)}, u32[]{:S(2)}) copy-start(bf16[8,512,512]{2,1,0:T(8,128)(2,1)} %gather_fusion) | copy-start | bytes 12582916
  349.1 3.6 collective-permute-start.14
